TPU v7x, 256 devices: a whole 4x4x8 slice. The times are simulated.
256 devices in a mesh: grp: 8 (over z), sp: 32 (over y, x, core).
Axes of the slice: x: 4, y: 4, z: 8, core: 2. Of those that a mesh axis runs over, the one named last changes fastest.
Arguments:
- queries: bfloat16 [65536, 4096], P(('grp', 'sp')), may hold values from -48 to 48
- keys: bfloat16 [65536, 4096], P(('grp', 'sp')), may hold values from -48 to 48
- values: bfloat16 [65536, 4096], P(('grp', 'sp')), may hold values from -6 to 6
- clip_lengths: int32 [8, 16], P('grp'), may hold values from 1 to 1023, as said below
- clip_plan: int32 [8, 16], P('grp'), may hold values from 0 to 7
Outputs:
- attended: bfloat16 [65536, 4096], P(('grp', 'sp'))
Inputs may be any that keep to these rules, and one draw needn't show every extreme that they name: `clip_lengths`: each group's clips, in order, fill its 8192 source rows; the clips that one group sends to any one group are exactly 2 and hold exactly 1024 frames together.
All inputs are finite; a program needn't handle non-finite values.
Results may differ from a plain program's by a relative error of at most 0.0037.
Values may be sent and summed in bfloat16 or wider, within the bound.
A program may use at most 64 MiB of HBM per device.

v0:
```python
from functools import partial
import math

import jax
import jax.numpy as jnp
from jax import lax
from jax.sharding import PartitionSpec as P

HEAD_DIM = 128


def row_tables(lengths, destination, frames):
    clip_order = jnp.arange(lengths.shape[0], dtype=jnp.int32)
    earlier = clip_order[None, :] < clip_order[:, None]
    clip_start = jnp.sum(jnp.where(earlier, lengths[None, :], 0), axis=1)
    before = (destination[None, :] < destination[:, None]) | (
        destination[None, :] == destination[:, None]
    ) & earlier
    sorted_start = jnp.sum(jnp.where(before, lengths[None, :], 0), axis=1)
    positions = jnp.arange(frames, dtype=jnp.int32)[:, None]
    inside_sorted = (positions >= sorted_start[None, :]) & (
        positions < (sorted_start + lengths)[None, :]
    )
    source_row = jnp.sum(
        jnp.where(inside_sorted, clip_start[None, :] + positions - sorted_start[None, :], 0), axis=1
    )
    sorted_begin = jnp.sum(jnp.where(inside_sorted, sorted_start[None, :], 0), axis=1)
    inside_source = (positions >= clip_start[None, :]) & (
        positions < (clip_start + lengths)[None, :]
    )
    source_begin = jnp.sum(jnp.where(inside_source, clip_start[None, :], 0), axis=1)
    return (source_row, sorted_begin, source_begin)


def attend_window(query_rows, key_rows, value_rows, clip_begin, share_rows):
    frames, local_width = query_rows.shape
    head_local = local_width // HEAD_DIM
    block_rows = min(512, frames)
    key_span = min(share_rows + block_rows, frames)
    score_scale = 1.0 / math.sqrt(HEAD_DIM)

    def one_block(block_index):
        row_first = block_index * block_rows
        key_first = jnp.clip(row_first - share_rows, 0, frames - key_span)
        query_block = lax.dynamic_slice_in_dim(query_rows, row_first, block_rows, 0).reshape(
            block_rows, head_local, HEAD_DIM
        )
        key_block = lax.dynamic_slice_in_dim(key_rows, key_first, key_span, 0).reshape(
            key_span, head_local, HEAD_DIM
        )
        value_block = lax.dynamic_slice_in_dim(value_rows, key_first, key_span, 0).reshape(
            key_span, head_local, HEAD_DIM
        )
        begin_block = lax.dynamic_slice_in_dim(clip_begin, row_first, block_rows, 0)
        scores = (
            jnp.einsum("qnd,knd->nqk", query_block, key_block, preferred_element_type=jnp.float32)
            * score_scale
        )
        query_pos = row_first + jnp.arange(block_rows, dtype=jnp.int32)
        key_pos = key_first + jnp.arange(key_span, dtype=jnp.int32)
        allowed = (key_pos[None, :] >= begin_block[:, None]) & (
            key_pos[None, :] <= query_pos[:, None]
        )
        scores = jnp.where(allowed[None], scores, -jnp.inf)
        highest = jnp.max(scores, axis=-1, keepdims=True)
        weights = jnp.exp(scores - highest)
        totals = jnp.sum(weights, axis=-1)
        mixture = jnp.einsum(
            "nqk,knd->qnd",
            weights.astype(jnp.bfloat16),
            value_block,
            preferred_element_type=jnp.float32,
        )
        return (
            (mixture / jnp.transpose(totals)[:, :, None])
            .astype(jnp.bfloat16)
            .reshape(block_rows, local_width)
        )

    blocks = lax.map(one_block, jnp.arange(frames // block_rows, dtype=jnp.int32))
    return blocks.reshape(frames, local_width)


def per_device(queries, keys, values, clip_lengths, clip_plan):
    frame_rows = queries.shape[0]
    group_rows = frame_rows * lax.axis_size("sp")
    group_count = lax.axis_size("grp")
    share_rows = group_rows // group_count
    heads_query, heads_key, heads_value = (
        lax.all_to_all(queries, "sp", split_axis=1, concat_axis=0, tiled=True),
        lax.all_to_all(keys, "sp", split_axis=1, concat_axis=0, tiled=True),
        lax.all_to_all(values, "sp", split_axis=1, concat_axis=0, tiled=True),
    )
    local_width = heads_query.shape[1]
    source_row, sorted_begin, source_begin = row_tables(clip_lengths[0], clip_plan[0], group_rows)

    def regroup(array):
        return jnp.take(array, source_row, axis=0).reshape(group_count, share_rows, local_width)

    every_length, every_plan = (
        lax.all_gather(clip_lengths, "grp", axis=0, tiled=True),
        lax.all_gather(clip_plan, "grp", axis=0, tiled=True),
    )
    all_tables = jax.vmap(partial(row_tables, frames=group_rows))(every_length, every_plan)
    position = lax.axis_index("grp")
    begun = all_tables[1].reshape(group_count, group_count, share_rows)
    begun = lax.dynamic_index_in_dim(begun, position, 1, keepdims=False)
    offsets = (jnp.arange(group_count, dtype=jnp.int32) * share_rows)[:, None]
    clip_begin = (begun - position * share_rows + offsets).reshape(group_rows)
    moved_query, moved_key, moved_value = (
        lax.all_to_all(regroup(heads_query), "grp", split_axis=0, concat_axis=0, tiled=True),
        lax.all_to_all(regroup(heads_key), "grp", split_axis=0, concat_axis=0, tiled=True),
        lax.all_to_all(regroup(heads_value), "grp", split_axis=0, concat_axis=0, tiled=True),
    )
    attended = attend_window(
        moved_query.reshape(group_rows, local_width),
        moved_key.reshape(group_rows, local_width),
        moved_value.reshape(group_rows, local_width),
        clip_begin,
        share_rows,
    )
    result = lax.all_to_all(attended, "sp", split_axis=0, concat_axis=1, tiled=True)
    return result


def solution(mesh):
    in_specs = (
        P(("grp", "sp"), None),
        P(("grp", "sp"), None),
        P(("grp", "sp"), None),
        P("grp", None),
        P("grp", None),
    )
    out_specs = P(("grp", "sp"), None)
    return jax.shard_map(
        per_device, mesh=mesh, in_specs=in_specs, out_specs=out_specs, check_vma=False
    )
```

profile of v0, /device:TPU:98, one launch (start us, length us, event | category | flops | bytes accessed | tf_op | source)
XLA Modules:
  0.0 510.6 jit_solution(8455850384307821318)
XLA Ops:
  3.5 7.7 %all-to-all-start = ((bf16[256,32,128]{2,0,1:T(8,128)(2,1)}), bf16[256,32,128]{2,0,1:T(8,128)(2,1)}, u32[]{:S(2)}, u32[]{:S(2)}) async-start(bf16[256,32,128]{2,0,1:T(8,128)(2,1)} %copy_bitcast_fusion.2), calls=%async_computation | async-start | bytes 4194304 | tf_op jit(solution)/shard_map/all_to_all | solution.py:92
  11.2 3.5 copy_bitcast_fusion.1
  14.7 24.4 %all-to-all-done = bf16[256,32,128]{2,0,1:T(8,128)(2,1)} async-done(((bf16[256,32,128]{2,0,1:T(8,128)(2,1)}), bf16[256,32,128]{2,0,1:T(8,128)(2,1)}, u32[]{:S(2)}, u32[]{:S(2)}) %all-to-all-start) | async-done | bytes 2097184 | tf_op jit(solution)/shard_map/all_to_all | solution.py:92
  39.1 6.7 %all-to-all-start.2 = ((bf16[256,32,128]{2,0,1:T(8,128)(2,1)}), bf16[256,32,128]{2,0,1:T(8,128)(2,1)}, u32[]{:S(2)}, u32[]{:S(2)}) async-start(bf16[256,32,128]{2,0,1:T(8,128)(2,1)} %copy_bitcast_fusion.1), calls=%async_computation.2 | async-start | bytes 4194304 | tf_op jit(solution)/shard_map/all_to_all | solution.py:90
  45.8 3.5 copy_bitcast_fusion
  49.3 24.5 %all-to-all-done.2 = bf16[256,32,128]{2,0,1:T(8,128)(2,1)} async-done(((bf16[256,32,128]{2,0,1:T(8,128)(2,1)}), bf16[256,32,128]{2,0,1:T(8,128)(2,1)}, u32[]{:S(2)}, u32[]{:S(2)}) %all-to-all-start.2) | async-done | bytes 2097184 | tf_op jit(solution)/shard_map/all_to_all | solution.py:90
  73.8 6.7 %all-to-all-start.4 = ((bf16[256,32,128]{2,0,1:T(8,128)(2,1)}), bf16[256,32,128]{2,0,1:T(8,128)(2,1)}, u32[]{:S(2)}, u32[]{:S(2)}) async-start(bf16[256,32,128]{2,0,1:T(8,128)(2,1)} %copy_bitcast_fusion), calls=%async_computation.4 | async-start | bytes 4194304 | tf_op jit(solution)/shard_map/all_to_all | solution.py:91
  81.1 29.9 %gather_fusion = bf16[8192,128]{1,0:T(8,128)(2,1)} fusion(bf16[8192,128]{1,0:T(8,128)(2,1)} %bitcast.9, s32[8192]{0:T(1024)S(1)} %fusion.25), kind=kCustom, calls=%fused_computation.clone | custom fusion | bytes 4227072 | tf_op jit(solution)/shard_map/jit(_take)/gather | solution.py:98
  110.9 29.8 %gather_fusion.1 = bf16[8192,128]{1,0:T(8,128)(2,1)} fusion(bf16[8192,128]{1,0:T(8,128)(2,1)} %bitcast.18, s32[8192]{0:T(1024)S(1)} %fusion.25), kind=kCustom, calls=%fused_computation.1.clone | custom fusion | bytes 4227072 | tf_op jit(solution)/shard_map/jit(_take)/gather | solution.py:98
  140.8 30.1 %gather_fusion.2 = bf16[8192,128]{1,0:T(8,128)(2,1)} fusion(bf16[8192,128]{1,0:T(8,128)(2,1)} %bitcast.22, s32[8192]{0:T(1024)S(1)} %fusion.25), kind=kCustom, calls=%fused_computation.2.clone | custom fusion | bytes 4227072 | tf_op jit(solution)/shard_map/jit(_take)/gather | solution.py:98
  170.9 7.4 %broadcast_select_fusion = (bf16[8192,128]{1,0:T(8,128)(2,1)}, bf16[8192,128]{1,0:T(8,128)(2,1)S(1)}, bf16[8192,128]{1,0:T(8,128)(2,1)S(1)}) fusion(bf16[8192,128]{1,0:T(8,128)(2,1)} %gather_fusion.2, pred[8192]{0:T(1024)(128)(4,1)S(1)} %compare_and_fusion, bf16[8192,128]{1,0:T(8,128)(2,1)} %gather_fusion.1, bf16[8192,128]{1,0:T(8,128)(2,1)} %gather_fusion), kind=kLoop, calls=%fused_computation.29 | loop fusion | flops 3145728 | bytes 12591104 | tf_op jit(solution)/shard_map/jit(_take)/select_n | solution.py:98
  178.3 55.4 %all_to_all.91 = bf16[8,1024,128]{2,1,0:T(8,128)(2,1)} all-to-all(bf16[8,1024,128]{2,1,0:T(8,128)(2,1)S(1)} %bitcast.78), channel_id=1, replica_groups=mesh['grp'=8,'sp'=32] {'grp'}, dimensions={0} | all-to-all | bytes 4194304 | tf_op jit(solution)/shard_map/all_to_all | solution.py:113
  233.7 53.7 %all_to_all.92 = bf16[8,1024,128]{2,1,0:T(8,128)(2,1)} all-to-all(bf16[8,1024,128]{2,1,0:T(8,128)(2,1)S(1)} %bitcast.77), channel_id=1, replica_groups=mesh['grp'=8,'sp'=32] {'grp'}, dimensions={0} | all-to-all | bytes 4194304 | tf_op jit(solution)/shard_map/all_to_all | solution.py:111
  287.4 7.7 %all-to-all-start.5 = ((bf16[8,1024,128]{2,1,0:T(8,128)(2,1)}), bf16[8,1024,128]{2,1,0:T(8,128)(2,1)}, u32[]{:S(2)}, u32[]{:S(2)}) async-start(bf16[8,1024,128]{2,1,0:T(8,128)(2,1)} %bitcast.76), calls=%async_computation.5 | async-start | bytes 4194304 | tf_op jit(solution)/shard_map/all_to_all | solution.py:112
  295.1 52.7 %all-gather.1 = s32[8,1,16]{2,1,0:T(1,128)S(1)} all-gather(s32[1,1,16]{2,1,0:T(1,128)S(1)} %bitcast.89), channel_id=1, replica_groups=mesh['grp'=8,'sp'=32] {'grp'}, dimensions={0}, use_global_device_ids=true | all-gather | bytes 576 | tf_op jit(solution)/shard_map/all_gather | solution.py:101
  347.8 14.5 %all-gather = s32[8,1,16]{2,1,0:T(1,128)S(1)} all-gather(s32[1,1,16]{2,1,0:T(1,128)S(1)} %bitcast.87), channel_id=1, replica_groups=mesh['grp'=8,'sp'=32] {'grp'}, dimensions={0}, use_global_device_ids=true | all-gather | bytes 576 | tf_op jit(solution)/shard_map/all_gather | solution.py:102
  364.1 103.4 %while.12 = (s32[]{:T(128)}, bf16[16,512,128]{2,1,0:T(8,128)(2,1)}, s32[16]{0:T(128)S(1)}, bf16[8192,128]{1,0:T(8,128)(2,1)}, s32[8192]{0:T(1024)S(1)}, /*index=...) while((s32[]{:T(128)}, bf16[16,512,128]{2,1,0:T(8,128)(2,1)}, ...), condition=%wide.region_8.10_spmd, body=%wide.region_5.9_spmd.sunk | while | flops 410649600 | bytes 11043571 | solution.py:80
  365.4 2.0 fusion.38
  371.8 2.0 fusion.38
  378.3 2.0 fusion.38
  384.8 2.0 fusion.38
  391.2 2.0 fusion.38
  397.7 2.0 fusion.38
  404.1 2.0 fusion.38
  410.6 2.0 fusion.38
  417.1 2.0 fusion.38
  436.4 2.0 fusion.38
  449.4 2.0 fusion.38
  462.3 2.0 fusion.38
  467.5 34.9 %all_to_all.93 = bf16[32,256,128]{2,1,0:T(8,128)(2,1)} all-to-all(bf16[32,256,128]{2,1,0:T(8,128)(2,1)} %bitcast.81), channel_id=1, replica_groups=mesh['grp'=8,'sp'=32] {'sp'}, dimensions={0} | all-to-all | bytes 4194304 | tf_op jit(solution)/shard_map/all_to_all | solution.py:122
  502.4 4.1 copy.29
  506.5 4.1 copy.30
  (156 shorter events, 75.3 us)
Async XLA Ops:
  0.0 1.6 copy-start
  3.5 35.6 %all-to-all-start = ((bf16[256,32,128]{2,0,1:T(8,128)(2,1)}), bf16[256,32,128]{2,0,1:T(8,128)(2,1)}, u32[]{:S(2)}, u32[]{:S(2)}) async-start(bf16[256,32,128]{2,0,1:T(8,128)(2,1)} %copy_bitcast_fusion.2), calls=%async_computation | async-start | bytes 4194304 | tf_op jit(solution)/shard_map/all_to_all | solution.py:92
  39.1 34.7 %all-to-all-start.2 = ((bf16[256,32,128]{2,0,1:T(8,128)(2,1)}), bf16[256,32,128]{2,0,1:T(8,128)(2,1)}, u32[]{:S(2)}, u32[]{:S(2)}) async-start(bf16[256,32,128]{2,0,1:T(8,128)(2,1)} %copy_bitcast_fusion.1), calls=%async_computation.2 | async-start | bytes 4194304 | tf_op jit(solution)/shard_map/all_to_all | solution.py:90
  49.3 31.2 %copy-start.1 = (s32[1,16]{1,0:T(1,128)S(1)}, s32[1,16]{1,0:T(1,128)}, u32[]{:S(2)}) copy-start(s32[1,16]{1,0:T(1,128)} %param.13) | copy-start | bytes 196
  49.3 31.2 %copy-start.2 = (s32[1,16]{1,0:T(1,128)S(1)}, s32[1,16]{1,0:T(1,128)}, u32[]{:S(2)}) copy-start(s32[1,16]{1,0:T(1,128)} %param.12) | copy-start | bytes 196
  73.8 67.0 %all-to-all-start.4 = ((bf16[256,32,128]{2,0,1:T(8,128)(2,1)}), bf16[256,32,128]{2,0,1:T(8,128)(2,1)}, u32[]{:S(2)}, u32[]{:S(2)}) async-start(bf16[256,32,128]{2,0,1:T(8,128)(2,1)} %copy_bitcast_fusion), calls=%async_computation.4 | async-start | bytes 4194304 | tf_op jit(solution)/shard_map/all_to_all | solution.py:91
  287.4 76.7 %all-to-all-start.5 = ((bf16[8,1024,128]{2,1,0:T(8,128)(2,1)}), bf16[8,1024,128]{2,1,0:T(8,128)(2,1)}, u32[]{:S(2)}, u32[]{:S(2)}) async-start(bf16[8,1024,128]{2,1,0:T(8,128)(2,1)} %bitcast.76), calls=%async_computation.5 | async-start | bytes 4194304 | tf_op jit(solution)/shard_map/all_to_all | solution.py:112
where the time goes:
time: 517 us; the launch traced here: 511 us
  blocking collectives  211 us (41%)
  local copies, waits for them, and re-layouts  132 us (26%)
  matrix products  61.2 us (12%)
  waiting for transfers between devices  48.9 us (9%)
  starting transfers between devices  28.8 us (6%)
  other arithmetic  18.8 us (4%)
  loops' own time  9.63 us (2%)
    gather x3, local copies, waits for them, and re-layouts, regroup(): jnp.take(array, source_row, axis=0)  89.9 us
    all_to_all x1, blocking collectives, per_device(): lax.all_to_all(regroup(heads_value), 'grp', split_axis=0, concat_axis=0,...  55.4 us
    all_to_all x1, blocking collectives, per_device(): lax.all_to_all(regroup(heads_query), 'grp', split_axis=0, concat_axis=0,...  53.7 us
    all_gather x1, blocking collectives, per_device(): lax.all_gather(clip_lengths, 'grp', axis=0, tiled=True)  52.7 us
    all_to_all x1, blocking collectives, per_device(): lax.all_to_all(attended, 'sp', split_axis=0, concat_axis=1, tiled=True)  34.9 us
    dot_general x16, matrix products, one_block(): jnp.einsum('qnd,knd->nqk', query_block, key_block, preferred_element_type...  32.1 us
    dot_general x16, matrix products, one_block(): jnp.einsum('nqk,knd->qnd', weights.astype(jnp.bfloat16), value_block, pre...  29 us
    all_to_all x1, waiting for transfers between devices, per_device(): lax.all_to_all(queries, 'sp', split_axis=1, concat_axis=0, tiled=True)  24.5 us
  transfers between devices with their start and end apart: 4, of which 2 were waited for; matrix products, arithmetic and copies ran while one was open for 14% of the time, Pallas kernels for 0%

commit v1 on v0

v1 whole, which is shorter than its diff:
```python
import functools
import math

import jax
import jax.numpy as jnp
from jax import lax
from jax.experimental import pallas as pl
from jax.experimental.pallas import tpu as pltpu
from jax.sharding import PartitionSpec as P

HEAD_DIM = 128
MESH = pl.DeviceIdType.MESH
STRIDE = 11
MASKED = -1.0e30


def fused_kernel(
    groups,
    sp_size,
    lens_ref,
    plan_ref,
    q_hbm,
    k_hbm,
    v_hbm,
    out_hbm,
    q_all,
    k_all,
    v_all,
    begin_all,
    prob_all,
    inverse_all,
    mixed_all,
    sorted_all,
    placed_all,
    in_send,
    in_recv,
    z_send,
    z_recv,
    out_send,
    out_recv,
    own_sem,
):
    rows = q_hbm.shape[0]
    clips = lens_ref.shape[1]
    quarters = sp_size // groups
    share = rows * quarters
    frames = rows * sp_size
    window = share + rows
    group = lax.axis_index("grp")
    me = lax.axis_index("sp")

    barrier = pltpu.get_barrier_semaphore()

    @pl.loop(1, sp_size)
    def _(t):
        peer = lax.rem(me + t, sp_size)
        pl.semaphore_signal(barrier, inc=1, device_id=(group, peer), device_id_type=MESH)

    @pl.loop(1, groups)
    def _(t):
        peer = lax.rem(group + t, groups)
        pl.semaphore_signal(barrier, inc=1, device_id=(peer, me), device_id_type=MESH)

    pl.semaphore_wait(barrier, sp_size + groups - 2)

    def head_columns(array, head):
        return array.at[:, pl.ds(pl.multiple_of(head * HEAD_DIM, HEAD_DIM), HEAD_DIM)]

    stacks = ((k_hbm, k_all, quarters), (q_hbm, q_all, 0), (v_hbm, v_all, quarters))

    def send_head(index, head):
        source, stack, pad = stacks[index]
        pltpu.make_async_remote_copy(
            src_ref=head_columns(source, head),
            dst_ref=stack.at[pad + me],
            send_sem=in_send.at[index],
            recv_sem=in_recv.at[index, me],
            device_id=(group, head),
            device_id_type=MESH,
        ).start()

    for index in range(3):
        source, stack, pad = stacks[index]
        pltpu.make_async_copy(
            head_columns(source, me), stack.at[pad + me], in_recv.at[index, me]
        ).start()

    @pl.loop(1, sp_size)
    def _(t):
        head = lax.rem(me + t * STRIDE, sp_size)
        send_head(0, head)
        send_head(1, head)

    @pl.loop(1, sp_size)
    def _(t):
        send_head(2, lax.rem(me + t * STRIDE, sp_size))

    def wait_block(index, block):
        _, stack, pad = stacks[index]
        view = stack.at[pad + block]
        pltpu.make_async_copy(view, view, in_recv.at[index, block]).wait()

    lengths = [lens_ref[0, c] for c in range(clips)]
    plans = [plan_ref[0, c] for c in range(clips)]
    starts = []
    total = jnp.int32(0)
    for c in range(clips):
        starts.append(total)
        total = total + lengths[c]

    k_all[0:quarters] = jnp.zeros((quarters, rows, HEAD_DIM), k_all.dtype)
    v_all[0:quarters] = jnp.zeros((quarters, rows, HEAD_DIM), v_all.dtype)
    mixed_all[0:share, :] = jnp.zeros((share, HEAD_DIM), jnp.float32)
    mixed_all[share + frames :, :] = jnp.zeros((share, HEAD_DIM), jnp.float32)

    @pl.loop(0, sp_size)
    def _(block):
        first = block * rows
        position = first + lax.broadcasted_iota(jnp.int32, (rows, HEAD_DIM), 0)
        begin = jnp.zeros((rows, HEAD_DIM), jnp.int32)
        for c in range(1, clips):
            begin = jnp.where(position >= starts[c], starts[c], begin)
        begin_all[block] = begin - (first - share)

    scale = math.log2(math.e) / math.sqrt(HEAD_DIM)
    column = lax.broadcasted_iota(jnp.int32, (rows, window), 1)
    last_key = share + lax.broadcasted_iota(jnp.int32, (rows, window), 0)

    @pl.loop(0, sp_size)
    def _(block):
        wait_block(0, block)
        wait_block(1, block)
        window_keys = k_all[pl.ds(block, quarters + 1)].reshape(window, HEAD_DIM)
        scores = lax.dot_general(
            q_all[block],
            window_keys,
            (((1,), (1,)), ((), ())),
            preferred_element_type=jnp.float32,
        )
        begin = jnp.broadcast_to(begin_all[block][:, :1], (rows, window))
        allowed = (column >= begin) & (column <= last_key)
        scores = jnp.where(allowed, scores * scale, MASKED)
        highest = jnp.max(scores, axis=1, keepdims=True)
        weights = jnp.exp2(scores - highest)
        totals = jnp.sum(weights, axis=1, keepdims=True)
        inverse_all[block] = jnp.broadcast_to(1.0 / totals, (rows, HEAD_DIM))
        prob_all[block] = weights.astype(prob_all.dtype)

    @pl.loop(0, sp_size)
    def _(block):
        wait_block(2, block)
        window_values = v_all[pl.ds(block, quarters + 1)].reshape(window, HEAD_DIM)
        mixture = jnp.dot(prob_all[block], window_values, preferred_element_type=jnp.float32)
        mixed_all[pl.ds(pl.multiple_of(share + block * rows, rows), rows), :] = (
            mixture * inverse_all[block]
        )

    def pair_of(target):
        first_start = jnp.int32(0)
        first_length = jnp.int32(0)
        second_start = jnp.int32(0)
        for c in reversed(range(clips)):
            hit = plans[c] == target
            first_start = jnp.where(hit, starts[c], first_start)
            first_length = jnp.where(hit, lengths[c], first_length)
        for c in range(clips):
            second_start = jnp.where(plans[c] == target, starts[c], second_start)
        return first_start, first_length, second_start

    def step_of(step):
        quarter = lax.rem(step // groups + me, quarters)
        shift = lax.rem(5 * lax.rem(step, groups) + groups // 2, groups)
        return quarter, shift

    def z_copy(target, quarter):
        return pltpu.make_async_remote_copy(
            src_ref=sorted_all.at[target, quarter],
            dst_ref=placed_all.at[group, quarter],
            send_sem=z_send,
            recv_sem=z_recv.at[group, quarter],
            device_id=(target, me),
            device_id_type=MESH,
        )

    def deliver(block_ref, origin, quarter):
        holder = origin * quarters + quarter
        target = head_columns(out_hbm, me)

        @pl.when(holder == me)
        def _():
            pltpu.make_async_copy(block_ref, target, own_sem).start()

        @pl.when(holder != me)
        def _():
            pltpu.make_async_remote_copy(
                src_ref=block_ref,
                dst_ref=target,
                send_sem=out_send,
                recv_sem=out_recv,
                device_id=(group, holder),
                device_id_type=MESH,
            ).start()

    @pl.loop(0, groups * quarters)
    def _(step):
        quarter, shift = step_of(step)
        target = lax.rem(group + shift, groups)
        first_start, first_length, second_start = pair_of(target)
        offset = quarter * rows
        head = mixed_all[pl.ds(share + first_start + offset, rows), :]
        tail = mixed_all[pl.ds(share + second_start - first_length + offset, rows), :]
        position = offset + lax.broadcasted_iota(jnp.int32, (rows, HEAD_DIM), 0)
        merged = jnp.where(position < first_length, head, tail)
        sorted_all[target, quarter] = merged.astype(sorted_all.dtype)

        @pl.when(shift != 0)
        def _():
            z_copy(target, quarter).start()

        @pl.when(shift == 0)
        def _():
            deliver(sorted_all.at[target, quarter], group, quarter)

    @pl.loop(0, groups * quarters)
    def _(step):
        quarter, shift = step_of(step)
        origin = lax.rem(group + groups - shift, groups)

        @pl.when(shift != 0)
        def _():
            view = placed_all.at[origin, quarter]
            pltpu.make_async_copy(view, view, z_recv.at[origin, quarter]).wait()
            deliver(view, origin, quarter)

    own = head_columns(out_hbm, me)
    pltpu.make_async_copy(sorted_all.at[0, 0], own, own_sem).wait()
    most = out_hbm.at[:, pl.ds(0, (sp_size - 1) * HEAD_DIM)]
    pltpu.make_async_copy(most, most, out_recv).wait()
    others = q_all.at[pl.ds(0, sp_size - 1)]
    for index in range(3):
        pltpu.make_async_copy(others, others, in_send.at[index]).wait()
    pltpu.make_async_copy(others, others, out_send).wait()
    moved = placed_all.at[pl.ds(0, groups - 1)]
    pltpu.make_async_copy(moved, moved, z_send).wait()


def per_device(groups, sp_size, queries, keys, values, clip_lengths, clip_plan):
    rows, width = queries.shape
    quarters = sp_size // groups
    share = rows * quarters
    frames = rows * sp_size
    window = share + rows
    kind = queries.dtype
    hbm = pl.BlockSpec(memory_space=pltpu.HBM)
    smem = pl.BlockSpec(memory_space=pltpu.SMEM)
    return pl.pallas_call(
        functools.partial(fused_kernel, groups, sp_size),
        out_shape=jax.ShapeDtypeStruct((rows, width), kind),
        in_specs=[smem, smem, hbm, hbm, hbm],
        out_specs=hbm,
        scratch_shapes=[
            pltpu.VMEM((sp_size, rows, HEAD_DIM), kind),
            pltpu.VMEM((sp_size + quarters, rows, HEAD_DIM), kind),
            pltpu.VMEM((sp_size + quarters, rows, HEAD_DIM), kind),
            pltpu.VMEM((sp_size, rows, HEAD_DIM), jnp.int32),
            pltpu.VMEM((sp_size, rows, window), kind),
            pltpu.VMEM((sp_size, rows, HEAD_DIM), jnp.float32),
            pltpu.VMEM((share + frames + share, HEAD_DIM), jnp.float32),
            pltpu.VMEM((groups, quarters, rows, HEAD_DIM), kind),
            pltpu.VMEM((groups, quarters, rows, HEAD_DIM), kind),
            pltpu.SemaphoreType.DMA((3,)),
            pltpu.SemaphoreType.DMA((3, sp_size)),
            pltpu.SemaphoreType.DMA,
            pltpu.SemaphoreType.DMA((groups, quarters)),
            pltpu.SemaphoreType.DMA,
            pltpu.SemaphoreType.DMA,
            pltpu.SemaphoreType.DMA,
        ],
        compiler_params=pltpu.CompilerParams(
            collective_id=0, has_side_effects=True, vmem_limit_bytes=56 << 20
        ),
    )(clip_lengths, clip_plan, queries, keys, values)


def solution(mesh):
    rows = P(("grp", "sp"), None)
    return jax.shard_map(
        functools.partial(per_device, mesh.shape["grp"], mesh.shape["sp"]),
        mesh=mesh,
        in_specs=(rows, rows, rows, P("grp", None), P("grp", None)),
        out_specs=rows,
        check_vma=False,
    )
```

time: 517 us -> 151 us (0.29)
  the two profiles are of different devices: /device:TPU:98 before, /device:TPU:5 now
where the time goes in v1:
time: 151 us
  Pallas kernels  148 us (98%)
  local copies, waits for them, and re-layouts  3.13 us (2%)
    pallas_call x1, Pallas kernels, per_device(): pl.pallas_call(functools.partial(fused_kernel, groups, sp_size), out_shap...  148 us
    unnamed x1, local copies, waits for them, and re-layouts  3.13 us

profile of v1, /device:TPU:5, one launch (start us, length us, event | category | flops | bytes accessed | tf_op | source)
XLA Modules:
  0.0 151.3 jit_solution(459054802342621893)
XLA Ops:
  0.0 148.1 %shard_map.55 = bf16[256,4096]{1,0:T(8,128)(2,1)} custom-call(s32[1,16]{1,0:T(1,128)} %lens_ref.1, s32[1,16]{1,0:T(1,128)} %plan_ref.1, bf16[256,4096]{1,0:T(8,128)(2,1)} %q_hbm.1, bf16[256,4096]{1,0:T(8,128)(2,1)} %k_hbm.1, bf16[256,4096]{1,0:T(8,128)(2,1)} %v_hbm.1), custom_call_target="tpu_custom_call" | custom-call | tf_op jit(solution)/shard_map/pallas_call | solution.py:256
  148.2 3.1 %copy.7 = bf16[256,4096]{1,0:T(8,128)(2,1)} copy(bf16[256,4096]{1,0:T(8,128)(2,1)} %shard_map.55) | data formatting | bytes 4194304

commit v2 on v1

v2 whole, which is shorter than its diff:
```python
import functools
import math

import jax
import jax.numpy as jnp
from jax import lax
from jax.experimental import pallas as pl
from jax.experimental.pallas import tpu as pltpu
from jax.sharding import PartitionSpec as P

HEAD_DIM = 128
MESH = pl.DeviceIdType.MESH
PHASES = 2
CORES = 2
STRIDE = 5
MASKED = -1.0e30


def fused_kernel(
    groups,
    sp_size,
    lens_ref,
    plan_ref,
    q_hbm,
    k_hbm,
    v_hbm,
    out_hbm,
    q_all,
    k_all,
    v_all,
    begin_all,
    prob_all,
    inverse_all,
    mixed_first,
    mixed_second,
    sorted_all,
    placed_all,
    in_send,
    near_send,
    in_recv,
    halo_send,
    halo_recv,
    swap_send,
    swap_recv,
    z_send,
    z_recv,
    out_send,
    own_send,
    out_recv,
):
    rows = q_hbm.shape[0]
    clips = lens_ref.shape[1]
    quarters = sp_size // groups
    chips = sp_size // CORES
    blocks = sp_size // CORES
    held = groups // CORES
    share = rows * quarters
    frames = rows * sp_size
    half = rows * blocks
    window = share + rows
    group = lax.axis_index("grp")
    me = lax.axis_index("sp")
    chip = me // CORES
    core = lax.rem(me, CORES)
    sibling = chip * CORES + 1 - core

    barrier = pltpu.get_barrier_semaphore()

    @pl.loop(1, sp_size)
    def _(t):
        peer = lax.rem(me + t, sp_size)
        pl.semaphore_signal(barrier, inc=1, device_id=(group, peer), device_id_type=MESH)

    @pl.loop(1, groups)
    def _(t):
        peer = lax.rem(group + t, groups)
        pl.semaphore_signal(barrier, inc=1, device_id=(peer, me), device_id_type=MESH)
        pl.semaphore_signal(barrier, inc=1, device_id=(peer, sibling), device_id_type=MESH)

    pl.semaphore_wait(barrier, sp_size - 1 + 2 * (groups - 1))

    def head_columns(array, phase, holder):
        head = phase * chips + holder
        return array.at[:, pl.ds(pl.multiple_of(head * HEAD_DIM, HEAD_DIM), HEAD_DIM)]

    stacks = ((k_hbm, k_all, quarters), (q_hbm, q_all, 0), (v_hbm, v_all, quarters))
    taker = me // blocks
    place = lax.rem(me, blocks)

    def send_heads(phase, index):
        source, stack, pad = stacks[index]
        target = stack.at[phase, pad + place]
        arrived = in_recv.at[phase, index, place]

        @pl.loop(1, chips)
        def _(t):
            holder = lax.rem(chip + t * STRIDE, chips)
            pltpu.make_async_remote_copy(
                src_ref=head_columns(source, phase, holder),
                dst_ref=target,
                send_sem=in_send.at[phase, index],
                recv_sem=arrived,
                device_id=(group, holder * CORES + taker),
                device_id_type=MESH,
            ).start()

        own = head_columns(source, phase, chip)

        @pl.when(taker == core)
        def _():
            pltpu.make_async_copy(own, target, arrived).start()

        @pl.when(taker != core)
        def _():
            pltpu.make_async_remote_copy(
                src_ref=own,
                dst_ref=target,
                send_sem=near_send.at[phase, index],
                recv_sem=arrived,
                device_id=(group, sibling),
                device_id_type=MESH,
            ).start()

    def wait_block(phase, index, block):
        _, stack, pad = stacks[index]
        view = stack.at[phase, pad + block]
        pltpu.make_async_copy(view, view, in_recv.at[phase, index, block]).wait()

    def halo_copy(phase, which, stack):
        return pltpu.make_async_remote_copy(
            src_ref=stack.at[phase, pl.ds(blocks, quarters)],
            dst_ref=stack.at[phase, pl.ds(0, quarters)],
            send_sem=halo_send.at[phase, which],
            recv_sem=halo_recv.at[phase, which],
            device_id=(group, sibling),
            device_id_type=MESH,
        )

    def wait_stack(phase, index, which):
        stack = stacks[index][1]

        @pl.loop(blocks - quarters, blocks)
        def _(block):
            wait_block(phase, index, block)

        @pl.when(core == 0)
        def _():
            halo_copy(phase, which, stack).start()

        @pl.loop(0, blocks - quarters)
        def _(block):
            wait_block(phase, index, block)

    def wait_halo(phase, which, stack):
        @pl.when(core == 1)
        def _():
            halo_copy(phase, which, stack).wait_recv()

    lengths = [lens_ref[0, c] for c in range(clips)]
    plans = [plan_ref[0, c] for c in range(clips)]
    starts = []
    total = jnp.int32(0)
    for c in range(clips):
        starts.append(total)
        total = total + lengths[c]

    for index in range(3):
        send_heads(0, index)

    @pl.when(core == 0)
    def _():
        for phase in range(PHASES):
            for stack in (k_all, v_all):
                stack[phase, 0:quarters] = jnp.zeros((quarters, rows, HEAD_DIM), stack.dtype)

    mixed_all = (mixed_first, mixed_second)
    for mixed in mixed_all:
        mixed[0:share, :] = jnp.zeros((share, HEAD_DIM), jnp.float32)
        mixed[share + frames :, :] = jnp.zeros((share, HEAD_DIM), jnp.float32)

    @pl.loop(0, blocks)
    def _(block):
        first = core * half + block * rows
        position = first + lax.broadcasted_iota(jnp.int32, (rows, HEAD_DIM), 0)
        begin = jnp.zeros((rows, HEAD_DIM), jnp.int32)
        for c in range(1, clips):
            begin = jnp.where(position >= starts[c], starts[c], begin)
        begin_all[block] = begin - (first - share)

    scale = math.log2(math.e) / math.sqrt(HEAD_DIM)
    column = lax.broadcasted_iota(jnp.int32, (rows, window), 1)
    last_key = share + lax.broadcasted_iota(jnp.int32, (rows, window), 0)

    def weigh(phase):
        @pl.loop(0, blocks)
        def _(step):
            block = lax.rem(step + quarters, blocks)

            @pl.when(block == 0)
            def _():
                wait_halo(phase, 0, k_all)

            wait_block(phase, 1, block)
            window_keys = k_all[phase, pl.ds(block, quarters + 1)].reshape(window, HEAD_DIM)
            scores = lax.dot_general(
                q_all[phase, block],
                window_keys,
                (((1,), (1,)), ((), ())),
                preferred_element_type=jnp.float32,
            )
            begin = jnp.broadcast_to(begin_all[block][:, :1], (rows, window))
            allowed = (column >= begin) & (column <= last_key)
            scores = jnp.where(allowed, scores * scale, MASKED)
            highest = jnp.max(scores, axis=1, keepdims=True)
            weights = jnp.exp2(scores - highest)
            totals = jnp.sum(weights, axis=1, keepdims=True)
            inverse_all[block] = jnp.broadcast_to(1.0 / totals, (rows, HEAD_DIM))
            prob_all[block] = weights.astype(prob_all.dtype)

    def swap_copy(phase, first, count):
        view = mixed_all[phase].at[pl.ds(pl.multiple_of(share + first, rows), count), :]
        return pltpu.make_async_remote_copy(
            src_ref=view,
            dst_ref=view,
            send_sem=swap_send.at[phase],
            recv_sem=swap_recv.at[phase],
            device_id=(group, sibling),
            device_id_type=MESH,
        )

    def mix(phase):
        @pl.loop(0, blocks)
        def _(step):
            block = lax.rem(step + quarters, blocks)

            @pl.when(block == 0)
            def _():
                wait_halo(phase, 1, v_all)

            window_values = v_all[phase, pl.ds(block, quarters + 1)].reshape(window, HEAD_DIM)
            mixture = jnp.dot(prob_all[block], window_values, preferred_element_type=jnp.float32)
            first = core * half + block * rows
            mixed_all[phase][pl.ds(pl.multiple_of(share + first, rows), rows), :] = (
                mixture * inverse_all[block]
            )
            swap_copy(phase, first, rows).start()

    def pair_of(target):
        first_start = jnp.int32(0)
        first_length = jnp.int32(0)
        second_start = jnp.int32(0)
        for c in reversed(range(clips)):
            hit = plans[c] == target
            first_start = jnp.where(hit, starts[c], first_start)
            first_length = jnp.where(hit, lengths[c], first_length)
        for c in range(clips):
            second_start = jnp.where(plans[c] == target, starts[c], second_start)
        return first_start, first_length, second_start

    def deliver(phase, block_ref, holder, send_sem, begin):
        target = head_columns(out_hbm, phase, chip)
        remote = pltpu.make_async_remote_copy(
            src_ref=block_ref,
            dst_ref=target,
            send_sem=send_sem,
            recv_sem=out_recv,
            device_id=(group, holder),
            device_id_type=MESH,
        )

        @pl.when(holder != me)
        def _():
            if begin:
                remote.start()
            else:
                remote.wait_send()

        if begin:

            @pl.when(holder == me)
            def _():
                pltpu.make_async_copy(block_ref, target, out_recv).start()

    def regroup_step(step):
        quarter = lax.rem(step // held + chip, quarters)
        slot = lax.rem(step + group, held)
        return quarter, slot, core * held + slot

    def z_copy(phase, slot, target, quarter):
        return pltpu.make_async_remote_copy(
            src_ref=sorted_all.at[phase, slot, quarter],
            dst_ref=placed_all.at[phase, group, quarter // CORES],
            send_sem=z_send.at[phase, slot, quarter],
            recv_sem=z_recv.at[phase, group, quarter // CORES],
            device_id=(target, chip * CORES + lax.rem(quarter, CORES)),
            device_id_type=MESH,
        )

    def send_sorted(phase, begin):
        @pl.loop(0, held * quarters)
        def _(step):
            quarter, slot, target = regroup_step(step)
            if begin:
                first_start, first_length, second_start = pair_of(target)
                offset = quarter * rows
                head = mixed_all[phase][pl.ds(share + first_start + offset, rows), :]
                tail = mixed_all[phase][
                    pl.ds(share + second_start - first_length + offset, rows), :
                ]
                position = offset + lax.broadcasted_iota(jnp.int32, (rows, HEAD_DIM), 0)
                merged = jnp.where(position < first_length, head, tail)
                sorted_all[phase, slot, quarter] = merged.astype(sorted_all.dtype)

            @pl.when(target != group)
            def _():
                if begin:
                    z_copy(phase, slot, target, quarter).start()
                else:
                    z_copy(phase, slot, target, quarter).wait_send()

            @pl.when(target == group)
            def _():
                deliver(
                    phase,
                    sorted_all.at[phase, slot, quarter],
                    group * quarters + quarter,
                    own_send.at[phase, quarter],
                    begin,
                )

    def forward(phase, begin):
        rounds = quarters // CORES
        parity = lax.rem(core + chip, CORES)

        @pl.loop(0, rounds * (groups - 1))
        def _(step):
            turn = step // (groups - 1)
            near = lax.rem(step, groups - 1) + 1
            odd = lax.rem(near, 2)
            hops = (near + 1) // 2
            shift = odd * hops + (1 - odd) * (groups - hops)
            origin = lax.rem(group + shift, groups)
            quarter = lax.rem(parity + CORES * turn + chip, quarters)
            kept = quarter // CORES
            view = placed_all.at[phase, origin, kept]
            if begin:
                pltpu.make_async_copy(view, view, z_recv.at[phase, origin, kept]).wait()
            deliver(
                phase, view, origin * quarters + quarter, out_send.at[phase, origin, kept], begin
            )

    for phase in range(PHASES):
        wait_stack(phase, 0, 0)
        if phase + 1 < PHASES:
            for index in range(3):
                send_heads(phase + 1, index)
        weigh(phase)
        wait_stack(phase, 2, 1)
        mix(phase)
        swap_copy(phase, (1 - core) * half, half).wait_recv()
        send_sorted(phase, True)
    for phase in range(PHASES):
        forward(phase, True)

    for phase in range(PHASES):
        for index in range(3):
            others = q_all.at[phase, pl.ds(0, chips - 1)]
            pltpu.make_async_copy(others, others, in_send.at[phase, index]).wait()

            @pl.when(taker != core)
            def _():
                one = q_all.at[phase, 0]
                pltpu.make_async_copy(one, one, near_send.at[phase, index]).wait()

        @pl.when(core == 0)
        def _():
            halo_copy(phase, 0, k_all).wait_send()
            halo_copy(phase, 1, v_all).wait_send()

        swap_copy(phase, core * half, half).wait_send()
        send_sorted(phase, False)
        forward(phase, False)
    pltpu.make_async_copy(out_hbm, out_hbm, out_recv).wait()


def per_device(groups, sp_size, queries, keys, values, clip_lengths, clip_plan):
    rows, width = queries.shape
    quarters = sp_size // groups
    blocks = sp_size // CORES
    held = groups // CORES
    kept = quarters // CORES
    share = rows * quarters
    frames = rows * sp_size
    window = share + rows
    kind = queries.dtype
    hbm = pl.BlockSpec(memory_space=pltpu.HBM)
    smem = pl.BlockSpec(memory_space=pltpu.SMEM)
    dma = pltpu.SemaphoreType.DMA
    return pl.pallas_call(
        functools.partial(fused_kernel, groups, sp_size),
        out_shape=jax.ShapeDtypeStruct((rows, width), kind),
        in_specs=[smem, smem, hbm, hbm, hbm],
        out_specs=hbm,
        scratch_shapes=[
            pltpu.VMEM((PHASES, blocks, rows, HEAD_DIM), kind),
            pltpu.VMEM((PHASES, blocks + quarters, rows, HEAD_DIM), kind),
            pltpu.VMEM((PHASES, blocks + quarters, rows, HEAD_DIM), kind),
            pltpu.VMEM((blocks, rows, HEAD_DIM), jnp.int32),
            pltpu.VMEM((blocks, rows, window), kind),
            pltpu.VMEM((blocks, rows, HEAD_DIM), jnp.float32),
            pltpu.VMEM((share + frames + share, HEAD_DIM), jnp.float32),
            pltpu.VMEM((share + frames + share, HEAD_DIM), jnp.float32),
            pltpu.VMEM((PHASES, held, quarters, rows, HEAD_DIM), kind),
            pltpu.VMEM((PHASES, groups, kept, rows, HEAD_DIM), kind),
            dma((PHASES, 3)),
            dma((PHASES, 3)),
            dma((PHASES, 3, blocks)),
            dma((PHASES, 2)),
            dma((PHASES, 2)),
            dma((PHASES,)),
            dma((PHASES,)),
            dma((PHASES, held, quarters)),
            dma((PHASES, groups, kept)),
            dma((PHASES, groups, kept)),
            dma((PHASES, quarters)),
            dma,
        ],
        compiler_params=pltpu.CompilerParams(
            collective_id=0, has_side_effects=True, vmem_limit_bytes=56 << 20
        ),
    )(clip_lengths, clip_plan, queries, keys, values)


def solution(mesh):
    rows = P(("grp", "sp"), None)
    return jax.shard_map(
        functools.partial(per_device, mesh.shape["grp"], mesh.shape["sp"]),
        mesh=mesh,
        in_specs=(rows, rows, rows, P("grp", None), P("grp", None)),
        out_specs=rows,
        check_vma=False,
    )
```

time: 151 us -> 132 us (0.87)
  the two profiles are of different devices: /device:TPU:5 before, /device:TPU:205 now
where the time goes in v2:
time: 132 us; the launch traced here: 131 us
  Pallas kernels  128 us (97%)
  local copies, waits for them, and re-layouts  3.13 us (2%)
    pallas_call x1, Pallas kernels, per_device(): pl.pallas_call(functools.partial(fused_kernel, groups, sp_size), out_shap...  128 us
    unnamed x1, local copies, waits for them, and re-layouts  3.13 us

profile of v2, /device:TPU:205, one launch (start us, length us, event | category | flops | bytes accessed | tf_op | source)
XLA Modules:
  0.0 131.4 jit_solution(11026121451962695509)
XLA Ops:
  0.0 128.3 %shard_map.55 = bf16[256,4096]{1,0:T(8,128)(2,1)} custom-call(s32[1,16]{1,0:T(1,128)} %lens_ref.1, s32[1,16]{1,0:T(1,128)} %plan_ref.1, bf16[256,4096]{1,0:T(8,128)(2,1)} %q_hbm.1, bf16[256,4096]{1,0:T(8,128)(2,1)} %k_hbm.1, bf16[256,4096]{1,0:T(8,128)(2,1)} %v_hbm.1), custom_call_target="tpu_custom_call" | custom-call | tf_op jit(solution)/shard_map/pallas_call | solution.py:399
  128.3 3.1 %copy.7 = bf16[256,4096]{1,0:T(8,128)(2,1)} copy(bf16[256,4096]{1,0:T(8,128)(2,1)} %shard_map.55) | data formatting | bytes 4194304

commit v3 on v2

--- a/solution.py
+++ b/solution.py
@@ -355,12 +355,13 @@
             for index in range(3):
                 send_heads(phase + 1, index)
         weigh(phase)
+        if phase == 1:
+            forward(0, True)
         wait_stack(phase, 2, 1)
         mix(phase)
         swap_copy(phase, (1 - core) * half, half).wait_recv()
         send_sorted(phase, True)
-    for phase in range(PHASES):
-        forward(phase, True)
+    forward(1, True)
 
     for phase in range(PHASES):
         for index in range(3):

time: 132 us -> 128 us (0.970)
  the two profiles are of different devices: /device:TPU:205 before, /device:TPU:98 now
where the time goes in v3:
time: 128 us
  Pallas kernels  125 us (98%)
  local copies, waits for them, and re-layouts  3.13 us (2%)
    pallas_call x1, Pallas kernels, per_device(): pl.pallas_call(functools.partial(fused_kernel, groups, sp_size), out_shap...  125 us
    unnamed x1, local copies, waits for them, and re-layouts  3.13 us

profile of v3, /device:TPU:98, one launch (start us, length us, event | category | flops | bytes accessed | tf_op | source)
XLA Modules:
  0.0 127.9 jit_solution(9700758842520895183)
XLA Ops:
  0.0 124.8 %shard_map.55 = bf16[256,4096]{1,0:T(8,128)(2,1)} custom-call(s32[1,16]{1,0:T(1,128)} %lens_ref.1, s32[1,16]{1,0:T(1,128)} %plan_ref.1, bf16[256,4096]{1,0:T(8,128)(2,1)} %q_hbm.1, bf16[256,4096]{1,0:T(8,128)(2,1)} %k_hbm.1, bf16[256,4096]{1,0:T(8,128)(2,1)} %v_hbm.1), custom_call_target="tpu_custom_call" | custom-call | tf_op jit(solution)/shard_map/pallas_call | solution.py:400
  124.8 3.1 %copy.7 = bf16[256,4096]{1,0:T(8,128)(2,1)} copy(bf16[256,4096]{1,0:T(8,128)(2,1)} %shard_map.55) | data formatting | bytes 4194304

commit v4 on v3

--- a/solution.py
+++ b/solution.py
@@ -92,9 +92,9 @@
         target = stack.at[phase, pad + place]
         arrived = in_recv.at[phase, index, place]
 
-        @pl.loop(1, chips)
-        def _(t):
-            holder = lax.rem(chip + t * STRIDE, chips)
+        for dx, dy in [(2, 2), (2, 1), (1, 2), (2, -1), (-1, 2), (1, 1), (-1, -1), (1, -1), (-1, 1), (2, 0), (0, 2), (1, 0), (0, 1), (-1, 0), (0, -1)]:
+            sign = 1 - 2 * core if True else 1
+            holder = lax.rem(chip // 4 + sign * dy + 8, 4) * 4 + lax.rem(lax.rem(chip, 4) + sign * dx + 8, 4)
             pltpu.make_async_remote_copy(
                 src_ref=head_columns(source, phase, holder),
                 dst_ref=target,
@@ -186,6 +186,26 @@
         for c in range(1, clips):
             begin = jnp.where(position >= starts[c], starts[c], begin)
         begin_all[block] = begin - (first - share)
+
+    def pair_of(target):
+        first_start = jnp.int32(0)
+        first_length = jnp.int32(0)
+        second_start = jnp.int32(0)
+        for c in reversed(range(clips)):
+            hit = plans[c] == target
+            first_start = jnp.where(hit, starts[c], first_start)
+            first_length = jnp.where(hit, lengths[c], first_length)
+        for c in range(clips):
+            second_start = jnp.where(plans[c] == target, starts[c], second_start)
+        return first_start, first_length, second_start
+
+    pairs = [pair_of(core * held + slot) for slot in range(held)]
+
+    def pick(slot):
+        found = pairs[0]
+        for other in range(1, held):
+            found = [jnp.where(slot == other, a, b) for a, b in zip(pairs[other], found)]
+        return found
 
     scale = math.log2(math.e) / math.sqrt(HEAD_DIM)
     column = lax.broadcasted_iota(jnp.int32, (rows, window), 1)
@@ -245,18 +265,6 @@
             )
             swap_copy(phase, first, rows).start()
 
-    def pair_of(target):
-        first_start = jnp.int32(0)
-        first_length = jnp.int32(0)
-        second_start = jnp.int32(0)
-        for c in reversed(range(clips)):
-            hit = plans[c] == target
-            first_start = jnp.where(hit, starts[c], first_start)
-            first_length = jnp.where(hit, lengths[c], first_length)
-        for c in range(clips):
-            second_start = jnp.where(plans[c] == target, starts[c], second_start)
-        return first_start, first_length, second_start
-
     def deliver(phase, block_ref, holder, send_sem, begin):
         target = head_columns(out_hbm, phase, chip)
         remote = pltpu.make_async_remote_copy(
@@ -301,7 +309,7 @@
         def _(step):
             quarter, slot, target = regroup_step(step)
             if begin:
-                first_start, first_length, second_start = pair_of(target)
+                first_start, first_length, second_start = pick(slot)
                 offset = quarter * rows
                 head = mixed_all[phase][pl.ds(share + first_start + offset, rows), :]
                 tail = mixed_all[phase][

time: 128 us -> 127 us (level); the launches traced: 128 us -> 125 us
  Pallas kernels: 125 us -> 122 us
    pallas_call x1, Pallas kernels: 125 us -> 122 us  [per_device(): pl.pallas_call(functools.partial(fused_kernel, groups, sp_size), out_shap...]
where the time goes in v4:
time: 127 us; the launch traced here: 125 us
  Pallas kernels  122 us (96%)
  local copies, waits for them, and re-layouts  3.13 us (2%)
    pallas_call x1, Pallas kernels, per_device(): pl.pallas_call(functools.partial(fused_kernel, groups, sp_size), out_shap...  122 us
    unnamed x1, local copies, waits for them, and re-layouts  3.13 us

profile of v4, /device:TPU:98, one launch (start us, length us, event | category | flops | bytes accessed | tf_op | source)
XLA Modules:
  0.0 125.4 jit_solution(8693928410464940603)
XLA Ops:
  0.0 122.2 %shard_map.55 = bf16[256,4096]{1,0:T(8,128)(2,1)} custom-call(s32[1,16]{1,0:T(1,128)} %lens_ref.1, s32[1,16]{1,0:T(1,128)} %plan_ref.1, bf16[256,4096]{1,0:T(8,128)(2,1)} %q_hbm.1, bf16[256,4096]{1,0:T(8,128)(2,1)} %k_hbm.1, bf16[256,4096]{1,0:T(8,128)(2,1)} %v_hbm.1), custom_call_target="tpu_custom_call" | custom-call | tf_op jit(solution)/shard_map/pallas_call | solution.py:408
  122.3 3.1 %copy.7 = bf16[256,4096]{1,0:T(8,128)(2,1)} copy(bf16[256,4096]{1,0:T(8,128)(2,1)} %shard_map.55) | data formatting | bytes 4194304
